TPU v7x, 32 devices: a whole 2x2x4 slice. The times are simulated.
32 devices in a mesh: dp: 8 (over z, x), tensor: 4 (over y, core).
Axes of the slice: x: 2, y: 2, z: 4, core: 2. Of those that a mesh axis runs over, the one named last changes fastest.
Arguments:
- attn_out: bfloat16 [4096, 8192], P('dp', 'tensor'), may hold values from -6 to 6
- frozen_weight: bfloat16 [8192, 8192], P('tensor', 'dp'), may hold values from -0.0625 to 0.0625
- vector_bank: float32 [256, 256], replicated, may hold values from -0.18 to 0.18
- logits_a: float32 [16, 32, 2], P(None, 'tensor'), may hold values from -2 to 2
- index_a: int32 [16, 32, 2], P(None, 'tensor'), may hold values from 0 to 255, all different within a row
- logits_b: float32 [16, 32, 2], P(None, 'tensor'), may hold values from -2 to 2
- index_b: int32 [16, 32, 2], P(None, 'tensor'), may hold values from 0 to 255, all different within a row
- out_grad: bfloat16 [4096, 8192], P('dp'), may hold values from -6 to 6
Outputs:
- layer_out: bfloat16 [4096, 8192], P('dp', 'tensor')
- attn_grad: bfloat16 [4096, 8192], P('dp', 'tensor')
- bank_grad: float32 [256, 256], replicated
- logits_a_grad: float32 [16, 32, 2], P(None, 'tensor')
- logits_b_grad: float32 [16, 32, 2], P(None, 'tensor')
Inputs may be any that keep to these rules, and one draw needn't show every extreme that they name: `index_a`: the 2 entries of one sub-vector differ. `index_b`: the 2 entries of one sub-vector differ.
All inputs are finite; a program needn't handle non-finite values.
Results may differ from a plain program's by a relative error of at most 0.014.
Values may be sent and summed in bfloat16 or wider, within the bound.
A program may use at most 128 MiB of HBM per device.

v0:
```python
import jax
import jax.numpy as jnp
from jax import lax
from jax.sharding import PartitionSpec as P

adapter_scale = 2.0


def compose(logits, indices, vector_bank):
    weights = jax.nn.sigmoid(logits - logits[..., ::-1])
    levels = jnp.arange(vector_bank.shape[0], dtype=jnp.int32)
    picked = (indices[..., None] == levels).astype(jnp.float32)
    mixing = jnp.sum(picked * weights[..., None], axis=2)
    blocks = jnp.einsum("rjb,bc->rjc", mixing, vector_bank, precision=lax.Precision.HIGHEST)
    return (weights, picked, mixing, blocks.reshape(blocks.shape[0], -1))


def compose_back(grad_rows, weights, picked, mixing, vector_bank):
    blocks = grad_rows.reshape(mixing.shape[0], mixing.shape[1], -1)
    bank_part = jnp.einsum("rjb,rjc->bc", mixing, blocks, precision=lax.Precision.HIGHEST)
    projected = jnp.einsum("rjc,bc->rjb", blocks, vector_bank, precision=lax.Precision.HIGHEST)
    dots = jnp.sum(picked * projected[:, :, None, :], axis=3)
    logit_grad = weights * (dots - jnp.sum(weights * dots, axis=2, keepdims=True))
    return (bank_part, logit_grad)


def local(attn_out, frozen_weight, vector_bank, logits_a, index_a, logits_b, index_b, out_grad):
    weights_a, picked_a, mixing_a, rows_a = compose(logits_a, index_a, vector_bank)
    weights_b, picked_b, mixing_b, rows_b = compose(logits_b, index_b, vector_bank)
    down_a = rows_a.astype(jnp.bfloat16)
    up_b = rows_b.astype(jnp.bfloat16)
    own_width = up_b.shape[1]
    grad_cols = lax.dynamic_slice_in_dim(
        out_grad, lax.axis_index("tensor") * own_width, own_width, 1
    )
    low_part = jnp.dot(attn_out, down_a.T, preferred_element_type=jnp.float32)
    back_part = jnp.dot(grad_cols, up_b.T, preferred_element_type=jnp.float32)
    low_total = lax.psum(low_part, "tensor")
    low_bf = low_total.astype(jnp.bfloat16)
    gathered = lax.all_gather(frozen_weight, "dp", axis=1, tiled=True)
    partial_value = jnp.dot(attn_out, gathered, preferred_element_type=jnp.float32).astype(
        jnp.bfloat16
    )
    summed = lax.psum_scatter(partial_value, "tensor", scatter_dimension=1, tiled=True).astype(
        jnp.float32
    )
    layer_out = (
        summed + adapter_scale * jnp.dot(low_bf, up_b, preferred_element_type=jnp.float32)
    ).astype(jnp.bfloat16)
    back_total = lax.psum(back_part, "tensor")
    back_bf = back_total.astype(jnp.bfloat16)
    main = lax.dot_general(
        out_grad, gathered, (((1,), (1,)), ((), ())), preferred_element_type=jnp.float32
    )
    attn_grad = (
        main + adapter_scale * jnp.dot(back_bf, down_a, preferred_element_type=jnp.float32)
    ).astype(jnp.bfloat16)
    factor = adapter_scale / (attn_out.shape[0] * lax.axis_size("dp"))
    grad_a = factor * lax.dot_general(
        back_bf, attn_out, (((0,), (0,)), ((), ())), preferred_element_type=jnp.float32
    )
    grad_b = factor * lax.dot_general(
        low_bf, grad_cols, (((0,), (0,)), ((), ())), preferred_element_type=jnp.float32
    )
    bank_a, logit_grad_a = compose_back(grad_a, weights_a, picked_a, mixing_a, vector_bank)
    bank_b, logit_grad_b = compose_back(grad_b, weights_b, picked_b, mixing_b, vector_bank)
    bank_part = bank_a + bank_b
    bank_group = lax.psum(bank_part, "tensor")
    bank_grad, logits_a_grad, logits_b_grad = lax.psum(
        (bank_group, logit_grad_a, logit_grad_b), "dp"
    )
    return (layer_out, attn_grad, bank_grad, logits_a_grad, logits_b_grad)


def solution(mesh):
    return jax.shard_map(
        local,
        mesh=mesh,
        in_specs=(
            P("dp", "tensor"),
            P("tensor", "dp"),
            P(),
            P(None, "tensor", None),
            P(None, "tensor", None),
            P(None, "tensor", None),
            P(None, "tensor", None),
            P("dp", None),
        ),
        out_specs=(
            P("dp", "tensor"),
            P("dp", "tensor"),
            P(),
            P(None, "tensor", None),
            P(None, "tensor", None),
        ),
        check_vma=False,
    )
```

profile of v0, /device:TPU:0, one launch (start us, length us, event | category | flops | bytes accessed | tf_op | source)
XLA Modules:
  0.0 792.0 jit_solution(11416128303065305518)
XLA Ops:
  8.1 0.7 all-gather.2.cloned.1.call-update
  8.9 0.1 copy.36
  9.0 0.1 copy.33
  9.1 0.1 select_reduce_fusion.3
  9.2 0.3 convolution_convert_fusion.2
  9.5 0.2 copy-done
  9.7 0.6 convolution_bitcast_fusion.2
  10.4 12.9 %psum.42 = bf16[512,16]{0,1:T(8,128)(2,1)S(1)} all-reduce(f32[512,16]{0,1:T(8,128)S(1)} %convolution_bitcast_fusion.2), channel_id=1, replica_groups=mesh['dp'=8,'tensor'=4] {'tensor'}, use_global_device_ids=true, to_apply=%region_2.0 | all-reduce | flops 8192 | bytes 49152 | tf_op jit(solution)/shard_map/psum | solution.py:38
  23.3 2.1 convolution_multiply_fusion
  25.5 0.1 copy.37
  25.6 0.1 copy.40
  25.7 0.4 fusion.4
  26.1 0.2 select_reduce_fusion
  26.3 0.3 convolution_convert_fusion.1
  26.6 2.2 fusion.1
  28.9 11.5 %psum.43 = bf16[512,16]{0,1:T(8,128)(2,1)S(1)} all-reduce(f32[512,16]{0,1:T(8,128)S(1)} %fusion.1), channel_id=1, replica_groups=mesh['dp'=8,'tensor'=4] {'tensor'}, use_global_device_ids=true, to_apply=%region_4.0 | all-reduce | flops 8192 | bytes 49152 | tf_op jit(solution)/shard_map/psum | solution.py:50
  40.3 0.4 convolution_multiply_fusion.1
  40.8 0.4 convolution_bitcast_fusion
  41.2 1.1 fusion.3
  42.4 608.5 %all-gather.2.cloned.1.call-done = bf16[2048,8192]{1,0:T(8,128)(2,1)} async-done(((bf16[2048,1024]{1,0:T(8,128)(2,1)}), bf16[2048,8192]{1,0:T(8,128)(2,1)}) %all-gather.2.cloned.1.call-update) | async-done | bytes 33554448 | tf_op jit(solution)/shard_map/all_gather | solution.py:40
  650.8 25.3 %convolution_convert_fusion = bf16[512,8192]{1,0:T(8,128)(2,1)} fusion(bf16[512,2048]{1,0:T(8,128)(2,1)S(1)} %copy-done, bf16[2048,8192]{1,0:T(8,128)(2,1)} %all-gather.2.cloned.1.call-done), kind=kOutput, calls=%fused_computation | convolution fusion | flops 17184063488 | bytes 44040192 | tf_op jit(solution)/shard_map/dot_general | solution.py:41
  676.3 0.4 fusion.6
  676.7 0.2 select_reduce_fusion.1
  677.1 36.0 %all-reduce = (f32[16,8,2]{0,1,2:T(8,128)S(1)}, f32[16,8,2]{0,1,2:T(8,128)S(1)}) all-reduce(f32[16,8,2]{0,1,2:T(8,128)S(1)} %get-tuple-element.20, f32[16,8,2]{0,1,2:T(8,128)S(1)} %get-tuple-element.19), channel_id=1, replica_groups=mesh['dp'=8,'tensor'=4] {'dp'}, use_global_device_ids=true, to_apply=%region_9.0 | all-reduce | flops 512 | bytes 4096 | tf_op jit(solution)/shard_map/psum | solution.py:69
  713.1 0.6 copy.45
  713.7 0.6 copy.46
  714.3 24.3 %fusion.24 = f32[512,2048]{1,0:T(8,128)S(1)} fusion(bf16[512,8192]{1,0:T(8,128)(2,1)} %param.15, bf16[2048,8192]{1,0:T(8,128)(2,1)} %all-gather.2.cloned.1.call-done), kind=kOutput, calls=%fused_computation.46 | convolution fusion | flops 17179869184 | bytes 46137344 | tf_op jit(solution)/shard_map/dot_general | solution.py:52
  738.6 2.0 add_convert_fusion
  740.7 6.7 reduce-scatter.2.cloned.1.call-done
  747.4 3.6 add_convert_fusion.1
  751.1 31.9 %all-reduce.6.cloned.1.call-done = f32[256,256]{1,0:T(8,128)} async-done(((f32[256,256]{1,0:T(8,128)}), f32[256,256]{1,0:T(8,128)}) %all-reduce.6.cloned.1.call-update) | async-done | bytes 262160 | tf_op jit(solution)/shard_map/psum | solution.py:69
  782.9 1.7 copy.53
  (34 shorter events, 0.6 us)
Async XLA Ops:
  8.0 1.7 copy-start
  8.0 0.8 copy-start.5
  8.0 0.9 copy-start.3
  8.0 1.2 copy-start.2
  8.0 17.4 %copy-start.4 = (s32[16,8,2]{0,2,1:T(2,128)S(1)}, s32[16,8,2]{0,2,1:T(2,128)}, u32[]{:S(2)}) copy-start(s32[16,8,2]{0,2,1:T(2,128)} %param.14) | copy-start | bytes 3076
  8.1 17.5 %copy-start.6 = (f32[16,8,2]{0,2,1:T(2,128)S(1)}, f32[16,8,2]{0,2,1:T(2,128)}, u32[]{:S(2)}) copy-start(f32[16,8,2]{0,2,1:T(2,128)} %param.13) | copy-start | bytes 3076
  8.1 642.8 %all-gather.2.cloned.1.call-start = ((), (), s32[]{:S(2)}) async-start(), calls=%async_computation.1 | async-start | bytes 37748736 | tf_op jit(solution)/shard_map/all_gather | solution.py:40
  8.8 705.5 %all-reduce.4.cloned.1.call-start = ((), (), s32[]{:S(2)}) async-start(), calls=%async_computation.3 | async-start | bytes 524288 | tf_op jit(solution)/shard_map/psum | solution.py:68
  42.3 705.1 %reduce-scatter.2.cloned.1.call-start = ((), (), s32[]{:S(2)}) async-start(), calls=%async_computation.2 | async-start | bytes 10485760 | tf_op jit(solution)/shard_map/reduce_scatter | solution.py:44
  676.2 106.7 %all-reduce.6.cloned.1.call-start = ((), (), s32[]{:S(2)}) async-start(), calls=%async_computation.4 | async-start | bytes 524288 | tf_op jit(solution)/shard_map/psum | solution.py:69
  714.3 70.3 %copy-start.1 = (bf16[512,2048]{1,0:T(8,128)(2,1)S(1)}, bf16[512,2048]{1,0:T(8,128)(2,1)}, u32[]{:S(2)}) copy-start(bf16[512,2048]{1,0:T(8,128)(2,1)} %param.8) | copy-start | bytes 6291460
Sparse Core Ops, SparseCore 0:
  10.4 640.3 all-gather.1
  714.4 68.4 all-reduce.5
Sparse Core Ops, SparseCore 1:
  42.4 32.2 all-reduce.3
  676.3 71.1 reduce-scatter.1
where the time goes:
time: 792 us
  waiting for transfers between devices  648 us (82%)
  matrix products  63.7 us (8%)
  blocking collectives  60.4 us (8%)
  between operations  15.7 us (2%)
    all_gather x1, waiting for transfers between devices, local(): gathered = lax.all_gather(frozen_weight, 'dp', axis=1, tiled=True)  608 us
    psum x1, blocking collectives, local(): lax.psum((bank_group, logit_grad_a, logit_grad_b), 'dp')  36 us
    psum x1, waiting for transfers between devices, local(): lax.psum((bank_group, logit_grad_a, logit_grad_b), 'dp')  31.9 us
    dot_general x1, matrix products, local(): jnp.dot(attn_out, gathered, preferred_element_type=jnp.float32)  25.3 us
    dot_general x1, matrix products, local(): lax.dot_general(out_grad, gathered, (((1,), (1,)), ((), ())), preferred_e...  24.3 us
  transfers between devices with their start and end apart: 4, of which 3 were waited for; matrix products, arithmetic and copies ran while one was open for 8% of the time, Pallas kernels for 0%

commit v1 on v0

--- a/solution.py
+++ b/solution.py
@@ -2,6 +2,7 @@
 import jax.numpy as jnp
 from jax import lax
 from jax.sharding import PartitionSpec as P
+from jax.lax import all_gather
 
 adapter_scale = 2.0
 
@@ -37,7 +38,11 @@
     back_part = jnp.dot(grad_cols, up_b.T, preferred_element_type=jnp.float32)
     low_total = lax.psum(low_part, "tensor")
     low_bf = low_total.astype(jnp.bfloat16)
-    gathered = lax.all_gather(frozen_weight, "dp", axis=1, tiled=True)
+
+    def apply_patch(u, axis_name, row_dim):
+        return jnp.concatenate(all_gather(u, axis_name), row_dim)
+
+    gathered = apply_patch(frozen_weight, "dp", 1)
     partial_value = jnp.dot(attn_out, gathered, preferred_element_type=jnp.float32).astype(
         jnp.bfloat16
     )

time: 792 us -> 835 us (1.054)
  local copies, waits for them, and re-layouts: 3.69 us -> 45.9 us
    reshape x0 -> x1, local copies, waits for them, and re-layouts: none -> 42.2 us  [apply_patch(): return jnp.concatenate(all_gather(u, axis_name), row_dim)]
  transfers between devices with their start and end apart: 4 -> 4, of which waited for: 3 -> 3; matrix products, arithmetic and copies ran while one was open for 8% -> 13% of each run, Pallas kernels for 0% -> 0%
where the time goes in v1:
time: 835 us; the launch traced here: 833 us
  waiting for transfers between devices  648 us (78%)
  matrix products  62.5 us (7%)
  blocking collectives  60.3 us (7%)
  local copies, waits for them, and re-layouts  45.9 us (5%)
  between operations  15.7 us (2%)
    all_gather x1, waiting for transfers between devices, apply_patch(): return jnp.concatenate(all_gather(u, axis_name), row_dim)  608 us
    reshape x1, local copies, waits for them, and re-layouts, apply_patch(): return jnp.concatenate(all_gather(u, axis_name), row_dim)  42.2 us
    psum x1, blocking collectives, local(): lax.psum((bank_group, logit_grad_a, logit_grad_b), 'dp')  35.9 us
    psum x1, waiting for transfers between devices, local(): lax.psum((bank_group, logit_grad_a, logit_grad_b), 'dp')  31.9 us
    dot_general x1, matrix products, local(): jnp.dot(attn_out, gathered, preferred_element_type=jnp.float32)  24.3 us
    dot_general x1, matrix products, local(): lax.dot_general(out_grad, gathered, (((1,), (1,)), ((), ())), preferred_e...  24.2 us
  transfers between devices with their start and end apart: 4, of which 3 were waited for; matrix products, arithmetic and copies ran while one was open for 13% of the time, Pallas kernels for 0%

profile of v1, /device:TPU:0, one launch (start us, length us, event | category | flops | bytes accessed | tf_op | source)
XLA Modules:
  0.0 833.2 jit_solution(2812677365234545207)
XLA Ops:
  8.1 0.7 all-gather.3.cloned.1.call-update
  8.9 0.1 copy.55
  9.0 0.1 copy.52
  9.1 0.1 select_reduce_fusion.3
  9.2 0.3 convolution_convert_fusion.2
  9.5 0.2 copy-done
  9.7 0.6 convolution_bitcast_fusion.2
  10.4 12.9 %psum.42 = bf16[512,16]{0,1:T(8,128)(2,1)S(1)} all-reduce(f32[512,16]{0,1:T(8,128)S(1)} %convolution_bitcast_fusion.2), channel_id=1, replica_groups=mesh['dp'=8,'tensor'=4] {'tensor'}, use_global_device_ids=true, to_apply=%region_2.0 | all-reduce | flops 8192 | bytes 49152 | tf_op jit(solution)/shard_map/psum | solution.py:39
  23.3 2.1 convolution_multiply_fusion
  25.5 0.1 copy.56
  25.7 0.4 fusion.4
  26.1 0.2 select_reduce_fusion
  26.3 0.3 convolution_convert_fusion.1
  26.6 2.2 fusion.1
  28.9 11.5 %psum.43 = bf16[512,16]{0,1:T(8,128)(2,1)S(1)} all-reduce(f32[512,16]{0,1:T(8,128)S(1)} %fusion.1), channel_id=1, replica_groups=mesh['dp'=8,'tensor'=4] {'tensor'}, use_global_device_ids=true, to_apply=%region_4.0 | all-reduce | flops 8192 | bytes 49152 | tf_op jit(solution)/shard_map/psum | solution.py:55
  40.3 0.4 convolution_multiply_fusion.1
  40.8 0.4 convolution_bitcast_fusion
  41.2 1.1 fusion.3
  42.4 608.4 %all-gather.3.cloned.1.call-done = bf16[16384,1024]{1,0:T(8,128)(2,1)} async-done(((bf16[2048,1024]{1,0:T(8,128)(2,1)}), bf16[16384,1024]{1,0:T(8,128)(2,1)}) %all-gather.3.cloned.1.call-update) | async-done | bytes 33554448 | tf_op jit(solution)/shard_map/all_gather | solution.py:43
  650.8 42.2 %copy.51 = bf16[2048,8,1024]{0,2,1:T(8,128)(2,1)} copy(bf16[2048,8,1024]{2,0,1:T(8,128)(2,1)} %bitcast.51) | data formatting | bytes 67108864 | tf_op jit(solution)/shard_map/reshape | solution.py:43
  693.1 24.3 %convolution_convert_fusion = bf16[512,8192]{1,0:T(8,128)(2,1)} fusion(bf16[512,2048]{1,0:T(8,128)(2,1)S(1)} %copy-done, bf16[2048,8192]{0,1:T(8,128)(2,1)} %bitcast.52), kind=kOutput, calls=%fused_computation | convolution fusion | flops 17184063488 | bytes 44040192 | tf_op jit(solution)/shard_map/dot_general | solution.py:46
  717.5 0.4 fusion.6
  717.9 0.2 select_reduce_fusion.1
  718.3 35.9 %all-reduce = (f32[16,8,2]{0,1,2:T(8,128)S(1)}, f32[16,8,2]{0,1,2:T(8,128)S(1)}) all-reduce(f32[16,8,2]{0,1,2:T(8,128)S(1)} %get-tuple-element.20, f32[16,8,2]{0,1,2:T(8,128)S(1)} %get-tuple-element.19), channel_id=1, replica_groups=mesh['dp'=8,'tensor'=4] {'dp'}, use_global_device_ids=true, to_apply=%region_9.0 | all-reduce | flops 512 | bytes 4096 | tf_op jit(solution)/shard_map/psum | solution.py:74
  754.2 0.6 copy.64
  754.8 0.6 copy.65
  755.4 24.2 %fusion.24 = f32[512,2048]{1,0:T(8,128)S(1)} fusion(bf16[512,8192]{1,0:T(8,128)(2,1)} %param.15, bf16[2048,8192]{0,1:T(8,128)(2,1)} %bitcast.53), kind=kOutput, calls=%fused_computation.46 | convolution fusion | flops 17179869184 | bytes 46137344 | tf_op jit(solution)/shard_map/dot_general | solution.py:57
  779.7 2.0 add_convert_fusion
  781.7 6.9 reduce-scatter.2.cloned.1.call-done
  788.6 3.6 add_convert_fusion.1
  792.2 31.9 %all-reduce.6.cloned.1.call-done = f32[256,256]{1,0:T(8,128)} async-done(((f32[256,256]{1,0:T(8,128)}), f32[256,256]{1,0:T(8,128)}) %all-reduce.6.cloned.1.call-update) | async-done | bytes 262160 | tf_op jit(solution)/shard_map/psum | solution.py:74
  824.1 1.7 copy.72
  (35 shorter events, 0.7 us)
Async XLA Ops:
  8.0 1.7 copy-start
  8.0 0.8 copy-start.5
  8.0 0.9 copy-start.3
  8.0 1.2 copy-start.2
  8.0 17.4 %copy-start.4 = (s32[16,8,2]{0,2,1:T(2,128)S(1)}, s32[16,8,2]{0,2,1:T(2,128)}, u32[]{:S(2)}) copy-start(s32[16,8,2]{0,2,1:T(2,128)} %param.14) | copy-start | bytes 3076
  8.1 17.5 %copy-start.6 = (f32[16,8,2]{0,2,1:T(2,128)S(1)}, f32[16,8,2]{0,2,1:T(2,128)}, u32[]{:S(2)}) copy-start(f32[16,8,2]{0,2,1:T(2,128)} %param.13) | copy-start | bytes 3076
  8.1 642.8 %all-gather.3.cloned.1.call-start = ((), (), s32[]{:S(2)}) async-start(), calls=%async_computation.4 | async-start | bytes 37748736 | tf_op jit(solution)/shard_map/all_gather | solution.py:43
  8.8 746.6 %all-reduce.4.cloned.1.call-start = ((), (), s32[]{:S(2)}) async-start(), calls=%async_computation.2 | async-start | bytes 524288 | tf_op jit(solution)/shard_map/psum | solution.py:73
  42.3 746.3 %reduce-scatter.2.cloned.1.call-start = ((), (), s32[]{:S(2)}) async-start(), calls=%async_computation.1 | async-start | bytes 10485760 | tf_op jit(solution)/shard_map/reduce_scatter | solution.py:49
  717.4 106.7 %all-reduce.6.cloned.1.call-start = ((), (), s32[]{:S(2)}) async-start(), calls=%async_computation.3 | async-start | bytes 524288 | tf_op jit(solution)/shard_map/psum | solution.py:74
  755.4 70.3 %copy-start.1 = (bf16[512,2048]{1,0:T(8,128)(2,1)S(1)}, bf16[512,2048]{1,0:T(8,128)(2,1)}, u32[]{:S(2)}) copy-start(bf16[512,2048]{1,0:T(8,128)(2,1)} %param.8) | copy-start | bytes 6291460
Sparse Core Ops, SparseCore 0:
  10.4 640.3 all-gather.2
  755.6 68.5 all-reduce.5
Sparse Core Ops, SparseCore 1:
  42.4 32.2 all-reduce.3
  717.5 71.1 reduce-scatter.1
